TPU v7x, 256 devices: a whole 4x4x8 slice. The times are simulated.
256 devices in a mesh: section: 16 (over x, y), seq: 16 (over z, core).
Axes of the slice: x: 4, y: 4, z: 8, core: 2. Of those that a mesh axis runs over, the one named last changes fastest.
Arguments:
- inputs: bfloat16 [4, 8192, 1536], P(None, 'seq'), may hold values from -40 to 40
- weights: bfloat16 [2, 5, 1536, 1536], P(None, None, None, 'section'), may hold values from -0.0625 to 0.0625
- gains: float32 [2, 1536], replicated, may hold values from 0.1 to 1.9
Outputs:
- activations: bfloat16 [2, 4, 8192, 1536], P(None, None, 'seq', 'section')
All inputs are finite; a program needn't handle non-finite values.
Results may differ from a plain program's by a relative error of at most 0.0044.
Values may be sent and summed in bfloat16 or wider, within the bound.
No kernel may reach another device: no remote copies, remote signals or barrier semaphores. Data moves between devices by JAX's collectives and lax.ppermute only.
A program may use at most 128 MiB of HBM per device.

v0:
```python
import jax
import jax.numpy as jnp
from jax import lax
from jax.sharding import PartitionSpec as P


def with_halo(value, sides, width):
    for axis, dim in sides:
        count, length = (lax.axis_size(axis), value.shape[dim])
        up = [(i, (i + 1) % count) for i in range(count - 1)]
        down = [(j, i) for i, j in up]
        last = lax.slice_in_dim(value, length - width, length, axis=dim)
        initial = lax.slice_in_dim(value, 0, width, axis=dim)
        before = lax.ppermute(last, axis, up)
        after = lax.ppermute(initial, axis, down)
        value = jnp.concatenate([before, value, after], axis=dim)
    return value


def convolve(padded, kernel):
    count = padded.shape[1] - 4
    total = jnp.zeros((padded.shape[0], count, kernel.shape[2]), jnp.float32)
    for k in range(5):
        total = total + jnp.einsum(
            "brc,co->bro", padded[:, k : k + count], kernel[k], preferred_element_type=jnp.float32
        )
    return total


def normed(current, gain):
    values = current.astype(jnp.float32)
    scale = lax.rsqrt(jnp.mean(values * values, axis=-1, keepdims=True) + 1e-06)
    return jax.nn.gelu(values * scale * gain).astype(jnp.bfloat16)


def neighbours(hidden):
    return with_halo(hidden, (("seq", 1),), 2)


def local(inputs, weights, gains):
    share = weights.shape[3]
    begin = lax.axis_index("section") * share
    hidden = normed(inputs, gains[0])
    conv = convolve(neighbours(hidden), weights[0])
    own = lax.dynamic_slice_in_dim(inputs, begin, share, 2)
    current = (own.astype(jnp.float32) + conv).astype(jnp.bfloat16)
    results = [current]
    kernel = weights[1]
    whole = lax.all_gather(current, "section", axis=2, tiled=True)
    conv = convolve(neighbours(normed(whole, gains[1])), kernel)
    current = (current.astype(jnp.float32) + conv).astype(jnp.bfloat16)
    results.append(current)
    return jnp.stack(results, axis=0)


def solution(mesh):
    in_specs = (P(None, "seq", None), P(None, None, None, "section"), P())
    out_specs = P(None, None, "seq", "section")
    return jax.shard_map(local, mesh=mesh, in_specs=in_specs, out_specs=out_specs, check_vma=False)
```

profile of v0, /device:TPU:1, one launch (start us, length us, event | category | flops | bytes accessed | tf_op | source)
XLA Modules:
  0.0 165.4 jit_solution(3972784400976625223)
XLA Ops:
  6.5 4.2 %fusion = f32[4,512]{1,0:T(4,128)S(1)} fusion(bf16[4,512,1536]{2,1,0:T(8,128)(2,1)} %param.3), kind=kLoop, calls=%fused_computation.6 | loop fusion | flops 9435136 | bytes 6299648 | tf_op jit(solution)/shard_map/reduce_sum | solution.py:32
  10.8 0.3 copy-done.1
  11.2 5.8 %fusion.4 = bf16[4,512,1536]{2,1,0:T(8,128)(2,1)S(1)} fusion(bf16[4,512,1536]{2,1,0:T(8,128)(2,1)S(1)} %copy-done.1, f32[1536]{0:T(1024)S(1)} %get-tuple-element.6, f32[4,512]{1,0:T(4,128)S(1)} %add_rsqrt_fusion.1), kind=kLoop, calls=%fused_computation.10 | loop fusion | flops 37748736 | bytes 12597248 | tf_op jit(solution)/shard_map/convert_element_type | solution.py:33
  16.9 2.7 %copy-done.2 = bf16[4,512,1536]{2,1,0:T(8,128)(2,1)} copy-done((bf16[4,512,1536]{2,1,0:T(8,128)(2,1)}, bf16[4,512,1536]{2,1,0:T(8,128)(2,1)S(1)}, u32[]{:S(2)}) %copy-start.2) | copy-done | bytes 6291480
  19.6 4.9 %collective-permute-start = (bf16[4,2,1536]{2,1,0:T(2,128)(2,1)S(1)}, bf16[4,2,1536]{2,1,0:T(2,128)(2,1)S(1)}, u32[]{:S(2)}, u32[]{:S(2)}) collective-permute-start(bf16[4,2,1536]{2,1,0:T(2,128)(2,1)S(1)} %get-tuple-element.9), channel_id=1, source_target_pairs={{0,1},{1,2},{2,3},{3,4},{4,5},{5,6},{6,7},{7,8},{8,9},{9,10},{10,1... | collective-permute-start | bytes 73736 | tf_op jit(solution)/shard_map/ppermute | solution.py:14
  24.6 2.1 %collective-permute-start.1 = (bf16[4,2,1536]{2,1,0:T(2,128)(2,1)S(1)}, bf16[4,2,1536]{2,1,0:T(2,128)(2,1)S(1)}, u32[]{:S(2)}, u32[]{:S(2)}) collective-permute-start(bf16[4,2,1536]{2,1,0:T(2,128)(2,1)S(1)} %get-tuple-element.10), channel_id=1, source_target_pairs={{1,0},{2,1},{3,2},{4,3},{5,4},{6,5},{7,6},{8,7},{9,8},{10,9},{11,1... | collective-permute-start | bytes 73736 | tf_op jit(solution)/shard_map/ppermute | solution.py:15
  26.7 4.8 %fusion.83 = f32[4,512,96]{1,2,0:T(8,128)S(1)} fusion(bf16[4,512,1536]{2,1,0:T(8,128)(2,1)} %copy-done.2, bf16[2,5,1536,96]{2,3,1,0:T(8,128)(2,1)} %param.4), kind=kOutput, calls=%fused_computation.75 | convolution fusion | flops 603979776 | bytes 7372800 | tf_op jit(solution)/shard_map/brc,co->bro/dot_general | solution.py:24
  31.5 1.5 constant_dynamic-slice_fusion
  33.0 0.0 slice-start
  33.0 1.0 copy.18
  33.9 0.0 collective-permute-done.1
  33.9 4.8 %fusion.28 = f32[4,512,96]{1,2,0:T(8,128)S(1)} fusion(bf16[4,2,1536]{2,1,0:T(2,128)(2,1)S(1)} %collective-permute-done.1, bf16[4,512,1536]{2,1,0:T(8,128)(2,1)} %copy-done.2, bf16[2,5,1536,96]{2,3,1,0:T(8,128)(2,1)} %param.4), kind=kOutput, calls=%fused_computation.45 | convolution fusion | flops 616562688 | bytes 7397376 | tf_op jit(solution)/shard_map/brc,co->bro/dot_general | solution.py:24
  38.8 3.0 %fusion.30 = f32[4,512,96]{1,2,0:T(8,128)S(1)} fusion(bf16[4,512,1536]{2,1,0:T(8,128)(2,1)S(1)} %bitcast.58, bf16[4,2,1536]{2,1,0:T(2,128)(2,1)S(1)} %collective-permute-done, bf16[2,5,1536,96]{2,3,1,0:T(8,128)(2,1)} %param.4), kind=kOutput, calls=%fused_computation.48 | convolution fusion | flops 616562688 | bytes 7397376 | tf_op jit(solution)/shard_map/brc,co->bro/dot_general | solution.py:24
  41.8 0.0 copy-start.3
  41.8 3.1 %fusion.64 = f32[4,512,96]{1,2,0:T(8,128)S(1)} fusion(f32[4,512,96]{1,2,0:T(8,128)S(1)} %fusion.83, f32[4,512,96]{1,2,0:T(8,128)S(1)} %fusion.30, bf16[4,2,1536]{2,1,0:T(2,128)(2,1)S(1)} %collective-permute-done, bf16[4,512,1536]{2,1,0:T(8,128)(2,1)S(1)} %bitcast.58, bf16[2,5,1536,96]{2,3,1,0:T(8,128)(2,1)} %param.4), kind=kOutput, calls=%fused_computation.62 | convolution fusion | flops 616955904 | bytes 8970240 | tf_op jit(solution)/shard_map/brc,co->bro/dot_general | solution.py:24
  44.9 3.5 %fusion.67 = bf16[4,512,96]{1,2,0:T(8,128)(2,1)S(1)} fusion(f32[4,512,96]{1,2,0:T(8,128)S(1)} %fusion.28, f32[4,512,96]{1,2,0:T(8,128)S(1)} %fusion.64, bf16[4,512,1536]{2,1,0:T(8,128)(2,1)S(1)} %bitcast.58, bf16[4,2,1536]{2,1,0:T(2,128)(2,1)S(1)} %collective-permute-done.1, bf16[4,512,96]{1,2,0:T(8,128)(2,1)S(1)} %copy-done.3, ...), kind=kOutput, calls=%fused_computation.63 | convolution fusion | flops 617545728 | bytes 8970240 | tf_op jit(solution)/shard_map/brc,co->bro/dot_general | solution.py:24
  48.4 1.1 copy.16
  49.5 0.0 all-gather.2.cloned.1.call-update
  49.5 70.2 %all-gather.2.cloned.1.call-done = bf16[4,512,1536]{1,0,2:T(4,128)(2,1)} async-done(((bf16[4,512,96]{1,0,2:T(4,128)(2,1)}), bf16[4,512,1536]{1,0,2:T(4,128)(2,1)}) %all-gather.2.cloned.1.call-update) | async-done | bytes 6291472 | tf_op jit(solution)/shard_map/all_gather | solution.py:49
  119.7 10.6 %copy.17 = bf16[4,512,1536]{2,1,0:T(8,128)(2,1)} copy(bf16[4,512,1536]{1,0,2:T(4,128)(2,1)} %all-gather.2.cloned.1.call-done) | data formatting | bytes 12582912 | tf_op jit(solution)/shard_map/all_gather | solution.py:49
  130.3 4.2 %fusion.9 = f32[4,512]{1,0:T(4,128)S(1)} fusion(bf16[4,512,1536]{2,1,0:T(8,128)(2,1)} %copy.17), kind=kLoop, calls=%fused_computation.15 | loop fusion | flops 9435136 | bytes 6299648 | tf_op jit(solution)/shard_map/reduce_sum | solution.py:32
  134.6 0.4 copy-done
  134.9 5.8 %fusion.13 = bf16[4,512,1536]{2,1,0:T(8,128)(2,1)S(1)} fusion(bf16[4,512,1536]{2,1,0:T(8,128)(2,1)S(1)} %copy-done, f32[1536]{0:T(1024)S(1)} %get-tuple-element.5, f32[4,512]{1,0:T(4,128)S(1)} %add_rsqrt_fusion), kind=kLoop, calls=%fused_computation.19 | loop fusion | flops 37748736 | bytes 12597248 | tf_op jit(solution)/shard_map/convert_element_type | solution.py:33
  140.8 2.6 %collective-permute-start.3 = (bf16[4,2,1536]{2,1,0:T(2,128)(2,1)S(1)}, bf16[4,2,1536]{2,1,0:T(2,128)(2,1)S(1)}, u32[]{:S(2)}, u32[]{:S(2)}) collective-permute-start(bf16[4,2,1536]{2,1,0:T(2,128)(2,1)S(1)} %get-tuple-element.8), channel_id=1, source_target_pairs={{1,0},{2,1},{3,2},{4,3},{5,4},{6,5},{7,6},{8,7},{9,8},{10,9},{11,1... | collective-permute-start | bytes 73736 | tf_op jit(solution)/shard_map/ppermute | solution.py:15
  143.4 2.0 %fusion.77 = f32[4,512,96]{1,2,0:T(8,128)S(1)} fusion(bf16[4,512,1536]{2,1,0:T(8,128)(2,1)S(1)} %fusion.13, bf16[2,5,1536,96]{2,3,1,0:T(8,128)(2,1)S(1)} %copy-done.4), kind=kOutput, calls=%fused_computation.69 | convolution fusion | flops 603979776 | bytes 7372800 | tf_op jit(solution)/shard_map/brc,co->bro/dot_general | solution.py:24
  145.4 3.3 %collective-permute-start.2 = (bf16[4,2,1536]{2,1,0:T(2,128)(2,1)S(1)}, bf16[4,2,1536]{2,1,0:T(2,128)(2,1)S(1)}, u32[]{:S(2)}, u32[]{:S(2)}) collective-permute-start(bf16[4,2,1536]{2,1,0:T(2,128)(2,1)S(1)} %get-tuple-element.7), channel_id=1, source_target_pairs={{0,1},{1,2},{2,3},{3,4},{4,5},{5,6},{6,7},{7,8},{8,9},{9,10},{10,1... | collective-permute-start | bytes 73736 | tf_op jit(solution)/shard_map/ppermute | solution.py:14
  148.7 0.0 collective-permute-done.3
  148.7 2.1 %fusion.24 = f32[4,512,96]{1,2,0:T(8,128)S(1)} fusion(bf16[4,2,1536]{2,1,0:T(2,128)(2,1)S(1)} %collective-permute-done.3, bf16[4,512,1536]{2,1,0:T(8,128)(2,1)S(1)} %fusion.13, bf16[2,5,1536,96]{2,3,1,0:T(8,128)(2,1)S(1)} %copy-done.4), kind=kOutput, calls=%fused_computation.39 | convolution fusion | flops 616562688 | bytes 7397376 | tf_op jit(solution)/shard_map/brc,co->bro/dot_general | solution.py:24
  150.8 2.1 %fusion.26 = f32[4,512,96]{1,2,0:T(8,128)S(1)} fusion(bf16[4,512,1536]{2,1,0:T(8,128)(2,1)S(1)} %fusion.13, bf16[4,2,1536]{2,1,0:T(2,128)(2,1)S(1)} %collective-permute-done.2, bf16[2,5,1536,96]{2,3,1,0:T(8,128)(2,1)S(1)} %copy-done.4), kind=kOutput, calls=%fused_computation.42 | convolution fusion | flops 616562688 | bytes 7397376 | tf_op jit(solution)/shard_map/brc,co->bro/dot_general | solution.py:24
  152.9 2.1 %fusion.49 = f32[4,512,96]{1,2,0:T(8,128)S(1)} fusion(f32[4,512,96]{1,2,0:T(8,128)S(1)} %fusion.77, f32[4,512,96]{1,2,0:T(8,128)S(1)} %fusion.26, bf16[4,2,1536]{2,1,0:T(2,128)(2,1)S(1)} %collective-permute-done.2, bf16[4,512,1536]{2,1,0:T(8,128)(2,1)S(1)} %fusion.13, bf16[2,5,1536,96]{2,3,1,0:T(8,128)(2,1)S(1)} %copy-done.4), kind=kOutput, calls=%fused_computation.57 | convolution fusion | flops 616955904 | bytes 8970240 | tf_op jit(solution)/shard_map/brc,co->bro/dot_general | solution.py:24
  155.0 2.6 %fusion.70 = bf16[1,4,512,96]{2,3,1,0:T(8,128)(2,1)S(1)} fusion(bf16[4,512,96]{1,2,0:T(8,128)(2,1)S(1)} %fusion.67, f32[4,512,96]{1,2,0:T(8,128)S(1)} %fusion.24, f32[4,512,96]{1,2,0:T(8,128)S(1)} %fusion.49, bf16[4,512,1536]{2,1,0:T(8,128)(2,1)S(1)} %fusion.13, bf16[4,2,1536]{2,1,0:T(2,128)(2,1)S(1)} %collective-permute-done.3, ...), kind=kOutput, calls=%fused_computation.66 | convolution fusion | flops 617545728 | bytes 8970240 | tf_op jit(solution)/shard_map/brc,co->bro/dot_general | solution.py:24
  157.6 0.9 pad_maximum_fusion.8
  (20 shorter events, 0.2 us)
Async XLA Ops:
  6.5 4.3 %copy-start.5 = (f32[2,1536]{1,0:T(2,128)S(1)}, f32[2,1536]{1,0:T(2,128)}, u32[]{:S(2)}) copy-start(f32[2,1536]{1,0:T(2,128)} %param.5) | copy-start | bytes 36868
  6.5 113.2 %all-gather.2.cloned.1.call-start = ((), (), s32[]{:S(2)}) async-start(), calls=%async_computation | async-start | bytes 6684672 | tf_op jit(solution)/shard_map/all_gather | solution.py:49
  6.5 4.6 %copy-start.1 = (bf16[4,512,1536]{2,1,0:T(8,128)(2,1)S(1)}, bf16[4,512,1536]{2,1,0:T(8,128)(2,1)}, u32[]{:S(2)}) copy-start(bf16[4,512,1536]{2,1,0:T(8,128)(2,1)} %param.3) | copy-start | bytes 18874372
  16.9 2.7 %copy-start.2 = (bf16[4,512,1536]{2,1,0:T(8,128)(2,1)}, bf16[4,512,1536]{2,1,0:T(8,128)(2,1)S(1)}, u32[]{:S(2)}) copy-start(bf16[4,512,1536]{2,1,0:T(8,128)(2,1)S(1)} %fusion.4) | copy-start | bytes 18874372
  19.6 19.1 %collective-permute-start = (bf16[4,2,1536]{2,1,0:T(2,128)(2,1)S(1)}, bf16[4,2,1536]{2,1,0:T(2,128)(2,1)S(1)}, u32[]{:S(2)}, u32[]{:S(2)}) collective-permute-start(bf16[4,2,1536]{2,1,0:T(2,128)(2,1)S(1)} %get-tuple-element.9), channel_id=1, source_target_pairs={{0,1},{1,2},{2,3},{3,4},{4,5},{5,6},{6,7},{7,8},{8,9},{9,10},{10,1... | collective-permute-start | bytes 73736 | tf_op jit(solution)/shard_map/ppermute | solution.py:14
  24.6 9.3 %collective-permute-start.1 = (bf16[4,2,1536]{2,1,0:T(2,128)(2,1)S(1)}, bf16[4,2,1536]{2,1,0:T(2,128)(2,1)S(1)}, u32[]{:S(2)}, u32[]{:S(2)}) collective-permute-start(bf16[4,2,1536]{2,1,0:T(2,128)(2,1)S(1)} %get-tuple-element.10), channel_id=1, source_target_pairs={{1,0},{2,1},{3,2},{4,3},{5,4},{6,5},{7,6},{8,7},{9,8},{10,9},{11,1... | collective-permute-start | bytes 73736 | tf_op jit(solution)/shard_map/ppermute | solution.py:15
  33.0 5.8 %slice-start = ((s8[6291456]{0:T(1024)(128)(4,1)}), s8[2097152]{0:T(1024)(128)(4,1)S(1)}, s32[]{:S(2)}) async-start(s8[6291456]{0:T(1024)(128)(4,1)} %bitcast.57), calls=%async_computation.1 | async-start | bytes 4194304
  33.9 4.9 %slice-start.1 = ((s8[6291456]{0:T(1024)(128)(4,1)}), s8[4194304]{0:T(1024)(128)(4,1)S(1)}, s32[]{:S(2)}) async-start(s8[6291456]{0:T(1024)(128)(4,1)} %bitcast.57), calls=%async_computation.2 | async-start | bytes 8388608
  41.8 3.1 %copy-start.3 = (bf16[4,512,96]{1,2,0:T(8,128)(2,1)S(1)}, bf16[4,512,96]{1,2,0:T(8,128)(2,1)}, u32[]{:S(2)}) copy-start(bf16[4,512,96]{1,2,0:T(8,128)(2,1)} %copy.18) | copy-start | bytes 1179652
  130.3 4.6 %copy-start = (bf16[4,512,1536]{2,1,0:T(8,128)(2,1)S(1)}, bf16[4,512,1536]{2,1,0:T(8,128)(2,1)}, u32[]{:S(2)}) copy-start(bf16[4,512,1536]{2,1,0:T(8,128)(2,1)} %copy.17) | copy-start | bytes 18874372
  134.9 8.4 %copy-start.4 = (bf16[2,5,1536,96]{2,3,1,0:T(8,128)(2,1)S(1)}, bf16[2,5,1536,96]{2,3,1,0:T(8,128)(2,1)}, u32[]{:S(2)}) copy-start(bf16[2,5,1536,96]{2,3,1,0:T(8,128)(2,1)} %param.4) | copy-start | bytes 8847364
  140.8 7.9 %collective-permute-start.3 = (bf16[4,2,1536]{2,1,0:T(2,128)(2,1)S(1)}, bf16[4,2,1536]{2,1,0:T(2,128)(2,1)S(1)}, u32[]{:S(2)}, u32[]{:S(2)}) collective-permute-start(bf16[4,2,1536]{2,1,0:T(2,128)(2,1)S(1)} %get-tuple-element.8), channel_id=1, source_target_pairs={{1,0},{2,1},{3,2},{4,3},{5,4},{6,5},{7,6},{8,7},{9,8},{10,9},{11,1... | collective-permute-start | bytes 73736 | tf_op jit(solution)/shard_map/ppermute | solution.py:15
  145.4 5.4 %collective-permute-start.2 = (bf16[4,2,1536]{2,1,0:T(2,128)(2,1)S(1)}, bf16[4,2,1536]{2,1,0:T(2,128)(2,1)S(1)}, u32[]{:S(2)}, u32[]{:S(2)}) collective-permute-start(bf16[4,2,1536]{2,1,0:T(2,128)(2,1)S(1)} %get-tuple-element.7), channel_id=1, source_target_pairs={{0,1},{1,2},{2,3},{3,4},{4,5},{5,6},{6,7},{7,8},{8,9},{9,10},{10,1... | collective-permute-start | bytes 73736 | tf_op jit(solution)/shard_map/ppermute | solution.py:14
Sparse Core Ops, SparseCore 0:
  49.6 70.0 all-gather.1
where the time goes:
time: 166 us; the launch traced here: 165 us
  waiting for transfers between devices  70.3 us (42%)
  matrix products  30.1 us (18%)
  other arithmetic  21 us (13%)
  local copies, waits for them, and re-layouts  17.5 us (11%)
  between operations  13.6 us (8%)
  starting transfers between devices  12.9 us (8%)
    all_gather x1, waiting for transfers between devices, local(): whole = lax.all_gather(current, 'section', axis=2, tiled=True)  70.2 us
    dot_general x10, matrix products, convolve(): jnp.einsum('brc,co->bro', padded[:, k:k + count], kernel[k], preferred_el...  30.1 us
    convert_element_type x2, other arithmetic, normed(): return jax.nn.gelu(values * scale * gain).astype(jnp.bfloat16)  11.5 us
    all_gather x1, local copies, waits for them, and re-layouts, local(): whole = lax.all_gather(current, 'section', axis=2, tiled=True)  10.6 us
    reduce_sum x2, other arithmetic, normed(): scale = lax.rsqrt(jnp.mean(values * values, axis=-1, keepdims=True) + 1e-06)  8.46 us
    ppermute x2, starting transfers between devices, with_halo(): before = lax.ppermute(last, axis, up)  8.24 us
    ppermute x2, starting transfers between devices, with_halo(): after = lax.ppermute(initial, axis, down)  4.68 us
    unnamed x17, local copies, waits for them, and re-layouts  4.3 us
  transfers between devices with their start and end apart: 5, of which 1 were waited for; matrix products, arithmetic and copies ran while one was open for 10% of the time, Pallas kernels for 0%

commit v1 on v0

--- a/solution.py
+++ b/solution.py
@@ -2,6 +2,7 @@
 import jax.numpy as jnp
 from jax import lax
 from jax.sharding import PartitionSpec as P
+from jax.lax import all_to_all, axis_size
 
 
 def with_halo(value, sides, width):
@@ -46,7 +47,15 @@
     current = (own.astype(jnp.float32) + conv).astype(jnp.bfloat16)
     results = [current]
     kernel = weights[1]
-    whole = lax.all_gather(current, "section", axis=2, tiled=True)
+    whole = jnp.concatenate(
+        all_to_all(
+            jnp.stack([current] * axis_size("section"), axis=0),
+            split_axis=0,
+            axis_name="section",
+            concat_axis=0,
+        ),
+        axis=2,
+    )
     conv = convolve(neighbours(normed(whole, gains[1])), kernel)
     current = (current.astype(jnp.float32) + conv).astype(jnp.bfloat16)
     results.append(current)

time: 166 us -> 222 us (1.34); the launches traced: 165 us -> 218 us
  starting transfers between devices: 12.9 us -> 44.6 us
  other arithmetic: 21 us -> 38.9 us
  between operations: 13.6 us -> 0.27 us
  waiting for transfers between devices: 70.3 us -> 83.6 us
  local copies, waits for them, and re-layouts: 17.5 us -> 21.6 us
    all_to_all x0 -> x1, waiting for transfers between devices: none -> 83.6 us  [local(): all_to_all(jnp.stack([current] * axis_size('section'), axis=0), split_axi...]
    all_gather x1 -> x0, waiting for transfers between devices: 70.2 us -> none  [local(): whole = lax.all_gather(current, 'section', axis=2, tiled=True)]
    ppermute x2, starting transfers between devices: 8.24 us -> 33.7 us  [with_halo(): before = lax.ppermute(last, axis, up)]
    convert_element_type x1, local copies, waits for them, and re-layouts: 1.05 us -> 12.6 us  [normed(): values = current.astype(jnp.float32)]
    all_gather x1 -> x0, local copies, waits for them, and re-layouts: 10.6 us -> none  [local(): whole = lax.all_gather(current, 'section', axis=2, tiled=True)]
    convert_element_type x0 -> x1, other arithmetic: none -> 9.12 us  [normed(): values = current.astype(jnp.float32)]
    convert_element_type x2 -> x3, other arithmetic: 11.5 us -> 20.6 us  [normed(): return jax.nn.gelu(values * scale * gain).astype(jnp.bfloat16)]
    all_to_all x0 -> x1, starting transfers between devices: none -> 6.81 us  [local(): all_to_all(jnp.stack([current] * axis_size('section'), axis=0), split_axi...]
where the time goes in v1:
time: 222 us; the launch traced here: 218 us
  waiting for transfers between devices  83.6 us (38%)
  starting transfers between devices  44.6 us (20%)
  other arithmetic  38.9 us (18%)
  matrix products  29 us (13%)
  local copies, waits for them, and re-layouts  21.6 us (10%)
    all_to_all x1, waiting for transfers between devices, local(): all_to_all(jnp.stack([current] * axis_size('section'), axis=0), split_axi...  83.6 us
    ppermute x2, starting transfers between devices, with_halo(): before = lax.ppermute(last, axis, up)  33.7 us
    dot_general x10, matrix products, convolve(): jnp.einsum('brc,co->bro', padded[:, k:k + count], kernel[k], preferred_el...  29 us
    convert_element_type x3, other arithmetic, normed(): return jax.nn.gelu(values * scale * gain).astype(jnp.bfloat16)  20.6 us
    convert_element_type x1, local copies, waits for them, and re-layouts, normed(): values = current.astype(jnp.float32)  12.6 us
    convert_element_type x1, other arithmetic, normed(): values = current.astype(jnp.float32)  9.12 us
    reduce_sum x2, other arithmetic, normed(): scale = lax.rsqrt(jnp.mean(values * values, axis=-1, keepdims=True) + 1e-06)  8.27 us
    all_to_all x1, starting transfers between devices, local(): all_to_all(jnp.stack([current] * axis_size('section'), axis=0), split_axi...  6.81 us
  transfers between devices with their start and end apart: 5, of which 1 were waited for; matrix products, arithmetic and copies ran while one was open for 10% of the time, Pallas kernels for 0%

profile of v1, /device:TPU:1, one launch (start us, length us, event | category | flops | bytes accessed | tf_op | source)
XLA Modules:
  0.0 218.1 jit_solution(242186619643421064)
XLA Ops:
  0.0 4.2 %fusion = f32[4,512]{1,0:T(4,128)S(1)} fusion(bf16[4,512,1536]{2,1,0:T(8,128)(2,1)} %param.3), kind=kLoop, calls=%fused_computation.5 | loop fusion | flops 9435136 | bytes 6299648 | tf_op jit(solution)/shard_map/reduce_sum | solution.py:33
  4.3 0.3 copy-done
  4.6 5.8 %fusion.4 = bf16[4,512,1536]{2,1,0:T(8,128)(2,1)S(1)} fusion(bf16[4,512,1536]{2,1,0:T(8,128)(2,1)S(1)} %copy-done, f32[1536]{0:T(1024)S(1)} %get-tuple-element.6, f32[4,512]{1,0:T(4,128)S(1)} %add_rsqrt_fusion.1), kind=kLoop, calls=%fused_computation.9 | loop fusion | flops 37748736 | bytes 12597248 | tf_op jit(solution)/shard_map/convert_element_type | solution.py:34
  10.4 2.7 %copy-done.1 = bf16[4,512,1536]{2,1,0:T(8,128)(2,1)} copy-done((bf16[4,512,1536]{2,1,0:T(8,128)(2,1)}, bf16[4,512,1536]{2,1,0:T(8,128)(2,1)S(1)}, u32[]{:S(2)}) %copy-start.1) | copy-done | bytes 6291480
  13.1 4.9 %collective-permute-start = (bf16[4,2,1536]{2,1,0:T(2,128)(2,1)S(1)}, bf16[4,2,1536]{2,1,0:T(2,128)(2,1)S(1)}, u32[]{:S(2)}, u32[]{:S(2)}) collective-permute-start(bf16[4,2,1536]{2,1,0:T(2,128)(2,1)S(1)} %get-tuple-element.9), channel_id=1, source_target_pairs={{0,1},{1,2},{2,3},{3,4},{4,5},{5,6},{6,7},{7,8},{8,9},{9,10},{10,1... | collective-permute-start | bytes 73736 | tf_op jit(solution)/shard_map/ppermute | solution.py:15
  18.0 1.9 collective-permute-start.1
  20.0 4.8 %fusion.89 = f32[4,512,96]{1,2,0:T(8,128)S(1)} fusion(bf16[4,512,1536]{2,1,0:T(8,128)(2,1)} %copy-done.1, bf16[2,5,1536,96]{2,3,1,0:T(8,128)(2,1)} %param.4), kind=kOutput, calls=%fused_computation.82 | convolution fusion | flops 603979776 | bytes 7372800 | tf_op jit(solution)/shard_map/brc,co->bro/dot_general | solution.py:25
  24.8 1.5 constant_dynamic-slice_fusion
  26.2 1.0 copy.14
  27.2 4.9 %fusion.34 = f32[4,512,96]{1,2,0:T(8,128)S(1)} fusion(bf16[4,2,1536]{2,1,0:T(2,128)(2,1)S(1)} %collective-permute-done.1, bf16[4,512,1536]{2,1,0:T(8,128)(2,1)} %copy-done.1, bf16[2,5,1536,96]{2,3,1,0:T(8,128)(2,1)} %param.4), kind=kOutput, calls=%fused_computation.51 | convolution fusion | flops 616562688 | bytes 7397376 | tf_op jit(solution)/shard_map/brc,co->bro/dot_general | solution.py:25
  32.1 3.0 %fusion.36 = f32[4,512,96]{1,2,0:T(8,128)S(1)} fusion(bf16[4,512,1536]{2,1,0:T(8,128)(2,1)S(1)} %bitcast.65, bf16[4,2,1536]{2,1,0:T(2,128)(2,1)S(1)} %collective-permute-done, bf16[2,5,1536,96]{2,3,1,0:T(8,128)(2,1)} %param.4), kind=kOutput, calls=%fused_computation.54 | convolution fusion | flops 616562688 | bytes 7397376 | tf_op jit(solution)/shard_map/brc,co->bro/dot_general | solution.py:25
  35.1 0.0 copy-start.2
  35.1 3.1 %fusion.70 = f32[4,512,96]{1,2,0:T(8,128)S(1)} fusion(f32[4,512,96]{1,2,0:T(8,128)S(1)} %fusion.89, f32[4,512,96]{1,2,0:T(8,128)S(1)} %fusion.36, bf16[4,2,1536]{2,1,0:T(2,128)(2,1)S(1)} %collective-permute-done, bf16[4,512,1536]{2,1,0:T(8,128)(2,1)S(1)} %bitcast.65, bf16[2,5,1536,96]{2,3,1,0:T(8,128)(2,1)} %param.4), kind=kOutput, calls=%fused_computation.69 | convolution fusion | flops 616955904 | bytes 8970240 | tf_op jit(solution)/shard_map/brc,co->bro/dot_general | solution.py:25
  38.2 3.5 %fusion.73 = bf16[4,512,96]{1,2,0:T(8,128)(2,1)S(1)} fusion(f32[4,512,96]{1,2,0:T(8,128)S(1)} %fusion.34, f32[4,512,96]{1,2,0:T(8,128)S(1)} %fusion.70, bf16[4,512,1536]{2,1,0:T(8,128)(2,1)S(1)} %bitcast.65, bf16[4,2,1536]{2,1,0:T(2,128)(2,1)S(1)} %collective-permute-done.1, bf16[4,512,96]{1,2,0:T(8,128)(2,1)S(1)} %copy-done.2, ...), kind=kOutput, calls=%fused_computation.70 | convolution fusion | flops 617545728 | bytes 8970240 | tf_op jit(solution)/shard_map/brc,co->bro/dot_general | solution.py:25
  41.7 3.4 %stack.9 = bf16[16,4,512,96]{2,3,1,0:T(8,128)(2,1)} broadcast(bf16[4,512,96]{1,2,0:T(8,128)(2,1)S(1)} %fusion.73), dimensions={1,2,3} | broadcast | bytes 6684672 | tf_op jit(solution)/shard_map/stack | solution.py:52
  45.1 6.8 %all-to-all-start = ((bf16[16,4,512,96]{2,3,1,0:T(8,128)(2,1)}), bf16[16,4,512,96]{2,3,1,0:T(8,128)(2,1)}, u32[]{:S(2)}, u32[]{:S(2)}) async-start(bf16[16,4,512,96]{2,3,1,0:T(8,128)(2,1)} %stack.9), calls=%async_computation | async-start | bytes 12582912 | tf_op jit(solution)/shard_map/all_to_all | solution.py:51
  51.9 0.1 mul.122
  52.0 83.6 %all-to-all-done = bf16[16,4,512,96]{2,3,1,0:T(8,128)(2,1)} async-done(((bf16[16,4,512,96]{2,3,1,0:T(8,128)(2,1)}), bf16[16,4,512,96]{2,3,1,0:T(8,128)(2,1)}, u32[]{:S(2)}, u32[]{:S(2)}) %all-to-all-start) | async-done | bytes 6291488 | tf_op jit(solution)/shard_map/all_to_all | solution.py:51
  135.6 4.0 %multiply_reduce_fusion = f32[4,512]{1,0:T(4,128)S(1)} fusion(bf16[16,4,512,96]{2,3,1,0:T(8,128)(2,1)} %all-to-all-done), kind=kLoop, calls=%fused_computation.31 | loop fusion | flops 9435136 | bytes 6299648 | tf_op jit(solution)/shard_map/reduce_sum | solution.py:33
  139.6 9.1 %copy_convert_fusion = f32[16,4,512,96]{2,3,0,1:T(8,128)} fusion(bf16[16,4,512,96]{2,3,1,0:T(8,128)(2,1)} %all-to-all-done), kind=kLoop, calls=%fused_computation.56 | loop fusion | flops 3145728 | bytes 18874368 | tf_op jit(solution)/shard_map/convert_element_type | solution.py:32
  148.8 12.6 %copy.11 = f32[4,512,1536]{2,1,0:T(8,128)} copy(f32[4,512,1536]{1,2,0:T(8,128)} %bitcast.63) | data formatting | bytes 25165824 | tf_op jit(solution)/shard_map/convert_element_type | solution.py:32
  161.4 7.9 %fusion.17 = bf16[4,512,1536]{2,1,0:T(8,128)(2,1)S(1)} fusion(f32[4,512,1536]{2,1,0:T(8,128)} %copy.11, f32[1536]{0:T(1024)S(1)} %get-tuple-element.5, f32[4,512]{1,0:T(4,128)S(1)} %add_rsqrt_fusion), kind=kLoop, calls=%fused_computation.22 | loop fusion | flops 34603008 | bytes 18888704 | tf_op jit(solution)/shard_map/convert_element_type | solution.py:34
  169.3 0.0 copy-start.3
  169.3 2.2 %collective-permute-start.3 = (bf16[4,2,1536]{2,1,0:T(2,128)(2,1)S(1)}, bf16[4,2,1536]{2,1,0:T(2,128)(2,1)S(1)}, u32[]{:S(2)}, u32[]{:S(2)}) collective-permute-start(bf16[4,2,1536]{2,1,0:T(2,128)(2,1)S(1)} %get-tuple-element.8), channel_id=1, source_target_pairs={{1,0},{2,1},{3,2},{4,3},{5,4},{6,5},{7,6},{8,7},{9,8},{10,9},{11,1... | collective-permute-start | bytes 73736 | tf_op jit(solution)/shard_map/ppermute | solution.py:16
  171.5 6.9 %fusion.25 = bf16[4,512,16,96]{1,3,2,0:T(8,128)(2,1)S(1)} fusion(f32[16,96]{1,0:T(8,128)S(1)} %mul.122, f32[4,512]{1,0:T(4,128)S(1)} %add_rsqrt_fusion, bf16[16,4,512,96]{2,3,1,0:T(8,128)(2,1)} %all-to-all-done), kind=kLoop, calls=%fused_computation.30 | loop fusion | flops 37748736 | bytes 12597248 | tf_op jit(solution)/shard_map/convert_element_type | solution.py:34
  178.5 1.1 fusion.83
  179.6 28.8 %collective-permute-start.2 = (bf16[4,2,1536]{2,1,0:T(2,128)(2,1)S(1)}, bf16[4,2,1536]{2,1,0:T(2,128)(2,1)S(1)}, u32[]{:S(2)}, u32[]{:S(2)}) collective-permute-start(bf16[4,2,1536]{2,1,0:T(2,128)(2,1)S(1)} %get-tuple-element.7), channel_id=1, source_target_pairs={{0,1},{1,2},{2,3},{3,4},{4,5},{5,6},{6,7},{7,8},{8,9},{9,10},{10,1... | collective-permute-start | bytes 73736 | tf_op jit(solution)/shard_map/ppermute | solution.py:15
  208.4 2.0 fusion.30
  210.5 2.0 fusion.32
  212.5 2.1 fusion.55
  214.6 2.5 %fusion.76 = bf16[1,4,512,96]{2,3,1,0:T(8,128)(2,1)S(1)} fusion(bf16[4,512,96]{1,2,0:T(8,128)(2,1)S(1)} %fusion.73, f32[4,512,96]{1,2,0:T(8,128)S(1)} %fusion.30, f32[4,512,96]{1,2,0:T(8,128)S(1)} %fusion.55, bf16[4,512,1536]{2,1,0:T(8,128)(2,1)S(1)} %fusion.17, bf16[4,2,1536]{2,1,0:T(2,128)(2,1)S(1)} %collective-permute-done.3, ...), kind=kOutput, calls=%fused_computation.73 | convolution fusion | flops 617545728 | bytes 8970240 | tf_op jit(solution)/shard_map/brc,co->bro/dot_general | solution.py:25
  217.1 0.9 pad_maximum_fusion.8
  (20 shorter events, 0.2 us)
Async XLA Ops:
  0.0 4.6 %copy-start = (bf16[4,512,1536]{2,1,0:T(8,128)(2,1)S(1)}, bf16[4,512,1536]{2,1,0:T(8,128)(2,1)}, u32[]{:S(2)}) copy-start(bf16[4,512,1536]{2,1,0:T(8,128)(2,1)} %param.3) | copy-start | bytes 18874372
  0.0 4.3 %copy-start.4 = (f32[2,1536]{1,0:T(2,128)S(1)}, f32[2,1536]{1,0:T(2,128)}, u32[]{:S(2)}) copy-start(f32[2,1536]{1,0:T(2,128)} %param.5) | copy-start | bytes 36868
  10.4 2.7 %copy-start.1 = (bf16[4,512,1536]{2,1,0:T(8,128)(2,1)}, bf16[4,512,1536]{2,1,0:T(8,128)(2,1)S(1)}, u32[]{:S(2)}) copy-start(bf16[4,512,1536]{2,1,0:T(8,128)(2,1)S(1)} %fusion.4) | copy-start | bytes 18874372
  13.1 19.0 %collective-permute-start = (bf16[4,2,1536]{2,1,0:T(2,128)(2,1)S(1)}, bf16[4,2,1536]{2,1,0:T(2,128)(2,1)S(1)}, u32[]{:S(2)}, u32[]{:S(2)}) collective-permute-start(bf16[4,2,1536]{2,1,0:T(2,128)(2,1)S(1)} %get-tuple-element.9), channel_id=1, source_target_pairs={{0,1},{1,2},{2,3},{3,4},{4,5},{5,6},{6,7},{7,8},{8,9},{9,10},{10,1... | collective-permute-start | bytes 73736 | tf_op jit(solution)/shard_map/ppermute | solution.py:15
  18.0 9.2 %collective-permute-start.1 = (bf16[4,2,1536]{2,1,0:T(2,128)(2,1)S(1)}, bf16[4,2,1536]{2,1,0:T(2,128)(2,1)S(1)}, u32[]{:S(2)}, u32[]{:S(2)}) collective-permute-start(bf16[4,2,1536]{2,1,0:T(2,128)(2,1)S(1)} %get-tuple-element.10), channel_id=1, source_target_pairs={{1,0},{2,1},{3,2},{4,3},{5,4},{6,5},{7,6},{8,7},{9,8},{10,9},{11,1... | collective-permute-start | bytes 73736 | tf_op jit(solution)/shard_map/ppermute | solution.py:16
  26.2 5.8 %slice-start = ((s8[6291456]{0:T(1024)(128)(4,1)}), s8[2097152]{0:T(1024)(128)(4,1)S(1)}, s32[]{:S(2)}) async-start(s8[6291456]{0:T(1024)(128)(4,1)} %bitcast.64), calls=%async_computation.1 | async-start | bytes 4194304
  27.2 4.9 %slice-start.1 = ((s8[6291456]{0:T(1024)(128)(4,1)}), s8[4194304]{0:T(1024)(128)(4,1)S(1)}, s32[]{:S(2)}) async-start(s8[6291456]{0:T(1024)(128)(4,1)} %bitcast.64), calls=%async_computation.2 | async-start | bytes 8388608
  35.1 3.1 %copy-start.2 = (bf16[4,512,96]{1,2,0:T(8,128)(2,1)S(1)}, bf16[4,512,96]{1,2,0:T(8,128)(2,1)}, u32[]{:S(2)}) copy-start(bf16[4,512,96]{1,2,0:T(8,128)(2,1)} %copy.14) | copy-start | bytes 1179652
  45.1 90.5 %all-to-all-start = ((bf16[16,4,512,96]{2,3,1,0:T(8,128)(2,1)}), bf16[16,4,512,96]{2,3,1,0:T(8,128)(2,1)}, u32[]{:S(2)}, u32[]{:S(2)}) async-start(bf16[16,4,512,96]{2,3,1,0:T(8,128)(2,1)} %stack.9), calls=%async_computation | async-start | bytes 12582912 | tf_op jit(solution)/shard_map/all_to_all | solution.py:51
  169.3 9.2 %copy-start.3 = (bf16[2,5,1536,96]{2,3,1,0:T(8,128)(2,1)S(1)}, bf16[2,5,1536,96]{2,3,1,0:T(8,128)(2,1)}, u32[]{:S(2)}) copy-start(bf16[2,5,1536,96]{2,3,1,0:T(8,128)(2,1)} %param.4) | copy-start | bytes 8847364
  169.3 39.1 %collective-permute-start.3 = (bf16[4,2,1536]{2,1,0:T(2,128)(2,1)S(1)}, bf16[4,2,1536]{2,1,0:T(2,128)(2,1)S(1)}, u32[]{:S(2)}, u32[]{:S(2)}) collective-permute-start(bf16[4,2,1536]{2,1,0:T(2,128)(2,1)S(1)} %get-tuple-element.8), channel_id=1, source_target_pairs={{1,0},{2,1},{3,2},{4,3},{5,4},{6,5},{7,6},{8,7},{9,8},{10,9},{11,1... | collective-permute-start | bytes 73736 | tf_op jit(solution)/shard_map/ppermute | solution.py:16
  179.6 30.9 %collective-permute-start.2 = (bf16[4,2,1536]{2,1,0:T(2,128)(2,1)S(1)}, bf16[4,2,1536]{2,1,0:T(2,128)(2,1)S(1)}, u32[]{:S(2)}, u32[]{:S(2)}) collective-permute-start(bf16[4,2,1536]{2,1,0:T(2,128)(2,1)S(1)} %get-tuple-element.7), channel_id=1, source_target_pairs={{0,1},{1,2},{2,3},{3,4},{4,5},{5,6},{6,7},{7,8},{8,9},{9,10},{10,1... | collective-permute-start | bytes 73736 | tf_op jit(solution)/shard_map/ppermute | solution.py:15
